TPU v7x, 32 devices: a whole 2x2x4 slice. The times are simulated.
32 devices in a mesh: worker: 8 (over z, y), mp: 4 (over x, core).
Axes of the slice: x: 2, y: 2, z: 4, core: 2. Of those that a mesh axis runs over, the one named last changes fastest.
Arguments:
- gradients: bfloat16 [128, 1048576], P('worker', 'mp'), may hold values from -30 to 30
- center: float32 [1048576], P('mp'), may hold values from -6 to 6
- outside_sq: float32 [3, 128], P(None, 'worker'), may hold values from 209715.2 to 2097152
- radius: float32 [3], replicated, may hold values from 1.5 to 3
Outputs:
- new_center: float32 [1048576], P('mp')
- norms: float32 [128], P('worker')
All inputs are finite; a program needn't handle non-finite values.
Results may differ from a plain program's by a relative error of at most 0.0003.
Values sent between devices are 32-bit elements; how exact they have to be, the bound alone decides.
No kernel may reach another device: no remote copies, remote signals or barrier semaphores. Data moves between devices by JAX's collectives and lax.ppermute only.
A program may use at most 64 MiB of HBM per device.

v0:
```python
import functools

import jax
import jax.numpy as jnp
from jax import lax
from jax.experimental import pallas as pl
from jax.experimental.pallas import tpu as pltpu
from jax.sharding import PartitionSpec as P


LANES = 128
GROUP = 8
BLOCK = 32
VMEM_LIMIT = 24 << 20
SHARES = (1, 1)
SEND = ((3, 1, 2), (1, 2, 3))
BACK = ((3, 1, 2), (3, 1, 2))


def bits_of(size):
    count = size.bit_length() - 1
    assert 1 << count == size
    return count


def square_rows(x_ref, x_row, v_ref, v_row, rows, carry):
    unroll = min(64, rows)
    assert rows % unroll == 0 and unroll % 2 == 0

    def step(i, acc):
        acc = list(acc)
        for r in range(0, unroll, 2):
            row = v_row + i * unroll + r
            first = v_ref[pl.ds(row, 1), :]
            second = v_ref[pl.ds(row + 1, 1), :]
            at = (x_row + i * unroll + r) * GROUP
            for g in range(len(acc) // 2):
                both = x_ref[g, pl.ds(pl.multiple_of(at, 2 * GROUP), 2 * GROUP), :].astype(jnp.float32)
                a = both[:GROUP] - first
                b = both[GROUP:] - second
                acc[2 * g] = acc[2 * g] + a * a
                acc[2 * g + 1] = acc[2 * g + 1] + b * b
        return tuple(acc)

    return lax.fori_loop(0, rows // unroll, step, carry)


def zero_carry(groups):
    return tuple(jnp.zeros((GROUP, LANES), jnp.float32) for _ in range(2 * groups))


def store_carry(o_ref, acc, extra_ref, step):
    for g in range(len(acc) // 2):
        total = acc[2 * g] + acc[2 * g + 1]
        if step is not None:
            total = total + extra_ref[step, g * GROUP:(g + 1) * GROUP, :]
        o_ref[g * GROUP:(g + 1) * GROUP, :] = total


def load_body(chunks, parts, x_hbm, v_hbm, out_hbm, x_ref, v_ref, o_ref, extra_ref, out_ref, sems, sem):
    groups, total, _ = x_ref.shape
    rows = total // chunks
    per = rows // GROUP
    own = groups * GROUP

    def copies(c):
        window = pl.ds(c * rows, rows)
        part = pl.ds(c * per, per)
        return (
            pltpu.make_async_copy(x_hbm.at[:, window, :], x_ref.at[:, window, :], sems.at[0, c]),
            pltpu.make_async_copy(v_hbm.at[part, :], v_ref.at[part, :], sems.at[1, c]),
        )

    small = pltpu.make_async_copy(out_hbm, out_ref, sem)
    small.start()
    for c in range(chunks):
        for copy in copies(c):
            copy.start()
    acc = zero_carry(groups)
    for c in range(chunks):
        for copy in copies(c):
            copy.wait()
        acc = square_rows(x_ref, c * per, v_ref, c * per, per, acc)
    small.wait()
    corner = lax.broadcasted_iota(jnp.int32, (own, own), 0) == lax.broadcasted_iota(jnp.int32, (own, own), 1)
    lane = lax.broadcasted_iota(jnp.int32, (own, LANES), 1)
    for t in range(extra_ref.shape[0]):
        column = jnp.sum(jnp.where(corner, out_ref[t:t + 1, :], 0.0), axis=1, keepdims=True)
        extra_ref[t] = jnp.where(lane == 0, column / jnp.float32(parts), 0.0)
    store_carry(o_ref, acc, extra_ref, 0)


def square_body(offset, extra, x_ref, v_ref, *refs):
    acc = zero_carry(x_ref.shape[0])
    acc = square_rows(x_ref, pl.multiple_of(offset(), BLOCK), v_ref, 0, v_ref.shape[0], acc)
    store_carry(refs[-1], acc, refs[0], extra)


def build_weights(root, workers, devices, groups, s_ref, w_ref, k_ref):
    depth = BLOCK * GROUP
    ones = jnp.ones((GROUP, LANES), jnp.bfloat16)
    block = lax.broadcasted_iota(jnp.int32, (BLOCK, depth), 0)
    place = lax.broadcasted_iota(jnp.int32, (BLOCK, depth), 1)
    total = None
    for g in range(groups):
        one = s_ref[g * GROUP:(g + 1) * GROUP, :]
        two = jnp.concatenate([one, one], axis=0)
        high = two.astype(jnp.bfloat16)
        low = (two - high.astype(jnp.float32)).astype(jnp.bfloat16)
        squared = None
        for half in (high, low):
            tall = jnp.concatenate([half] * (BLOCK // 2), axis=0)
            part = lax.dot_general(ones, tall, (((1,), (1,)), ((), ())), preferred_element_type=jnp.float32)
            squared = part if squared is None else squared + part
        factor = jnp.minimum(jnp.float32(1.0), root / jnp.sqrt(squared))
        total = factor if total is None else total + factor
        factor = factor[0:1] / jnp.float32(workers)
        high = factor.astype(jnp.bfloat16).astype(jnp.float32)
        low = factor - high
        for h, half in enumerate((high, low)):
            w_ref[g, h * BLOCK:(h + 1) * BLOCK, :] = jnp.where(place // GROUP == block, half, 0.0).astype(jnp.bfloat16)
    share = jnp.sum(total, axis=1, keepdims=True) / jnp.float32(BLOCK * workers)
    k_ref[...] = jnp.broadcast_to(jnp.float32(1.0 / devices) - share, k_ref.shape)


def weigh_rows(off, relative, x_ref, v_ref, w_ref, k_ref, o_ref):
    groups = x_ref.shape[0]
    depth = BLOCK * GROUP
    keep = k_ref[0:1, :]
    steps = o_ref.shape[0] // (2 * BLOCK)
    base = pl.multiple_of(off, BLOCK)

    def step(i, _):
        at = base + i * 2 * BLOCK
        total = None
        for g in range(groups):
            left = x_ref[g, pl.ds(pl.multiple_of(at * GROUP, depth), depth), :]
            right = x_ref[g, pl.ds(pl.multiple_of(at * GROUP + depth, depth), depth), :]
            part = jnp.dot(w_ref[g], jnp.concatenate([left, right], axis=1), preferred_element_type=jnp.float32)
            total = part if total is None else total + part
        total = total[:BLOCK] + total[BLOCK:]
        o_at = i * 2 * BLOCK
        v_at = o_at if relative else at
        for h in range(2):
            old = v_ref[pl.ds(pl.multiple_of(v_at + h * BLOCK, BLOCK), BLOCK), :]
            o_ref[pl.ds(pl.multiple_of(o_at + h * BLOCK, BLOCK), BLOCK), :] = keep * old + total[:, h * LANES:(h + 1) * LANES]
        return 0

    lax.fori_loop(0, steps, step, 0, unroll=min(4, steps))


def first_body(offset, relative, step_at, devices, workers, root_total, radius_ref, x_ref, v_ref, s_ref, o_ref, w_ref, k_ref):
    build_weights(radius_ref[step_at] * root_total, workers, devices, x_ref.shape[0], s_ref, w_ref, k_ref)
    weigh_rows(offset(), relative, x_ref, v_ref, w_ref, k_ref, o_ref)


def weigh_body(offset, relative, x_ref, v_ref, w_ref, k_ref, o_ref):
    weigh_rows(offset(), relative, x_ref, v_ref, w_ref, k_ref, o_ref)


VM = pl.BlockSpec(memory_space=pltpu.VMEM)
SM = pl.BlockSpec(memory_space=pltpu.SMEM)
PARAMS = pltpu.CompilerParams(vmem_limit_bytes=VMEM_LIMIT)


def shards(gradients, center, outside_sq, radius):
    workers, size = gradients.shape
    iters = outside_sq.shape[0]
    devices = lax.axis_size("worker")
    parts = lax.axis_size("mp")
    levels = bits_of(devices)
    root_total = float(size * parts) ** 0.5
    groups = workers // GROUP
    rows = size // LANES
    x = gradients.reshape(groups, GROUP, rows, LANES).transpose(0, 2, 1, 3).reshape(groups, rows * GROUP, LANES)
    center = center.reshape(rows, LANES)

    streams = len(SHARES)
    heights = [rows * share // sum(SHARES) for share in SHARES]
    starts = [sum(heights[:s]) for s in range(streams)]

    def offset(s, r):
        return starts[s] + ((lax.axis_index("worker") & 3) ^ r) * (heights[s] >> 2)

    partial_shape = jax.ShapeDtypeStruct((workers, LANES), jnp.float32)

    chunks = 16
    x, center, partial, extra = pl.pallas_call(
        functools.partial(load_body, chunks, parts),
        out_shape=(
            jax.ShapeDtypeStruct(x.shape, x.dtype),
            jax.ShapeDtypeStruct(center.shape, center.dtype),
            partial_shape,
            jax.ShapeDtypeStruct((iters, workers, LANES), jnp.float32),
        ),
        in_specs=[pl.BlockSpec(memory_space=pltpu.HBM)] * 3,
        out_specs=(VM, VM, VM, VM),
        scratch_shapes=[
            pltpu.VMEM((iters, workers), jnp.float32), pltpu.SemaphoreType.DMA((2, chunks)), pltpu.SemaphoreType.DMA,
        ],
        compiler_params=PARAMS,
        name="load",
    )(*[pltpu.with_memory_space_constraint(a, pltpu.HBM) for a in (x, center, outside_sq)])

    def squares(s, r, value, step):
        more = [] if step is None else [extra]
        return pl.pallas_call(
            functools.partial(square_body, functools.partial(offset, s, r), step),
            out_shape=partial_shape, in_specs=[VM] * (2 + len(more)), out_specs=VM, compiler_params=PARAMS, name="squares",
        )(x, value, *more)

    weight_shape = jax.ShapeDtypeStruct((groups, 2 * BLOCK, BLOCK * GROUP), jnp.bfloat16)
    keep_shape = jax.ShapeDtypeStruct((GROUP, LANES), jnp.float32)

    def quarter_shape(s):
        return jax.ShapeDtypeStruct((heights[s] >> 2, LANES), jnp.float32)

    def weigh_first(s, r, value, relative, step, squared):
        body = functools.partial(
            first_body, functools.partial(offset, s, r), relative, step, devices, workers * devices, root_total
        )
        return pl.pallas_call(
            body, out_shape=(quarter_shape(s), weight_shape, keep_shape),
            in_specs=[SM, VM, VM, VM], out_specs=(VM, VM, VM), compiler_params=PARAMS, name="first",
        )(radius, x, value, squared)

    def weigh(s, r, value, relative, weights, keep):
        return pl.pallas_call(
            functools.partial(weigh_body, functools.partial(offset, s, r), relative),
            out_shape=quarter_shape(s), in_specs=[VM, VM, VM, VM], out_specs=VM, compiler_params=PARAMS, name="weigh",
        )(x, value, weights, keep)

    def over_parts(one):
        for mask in [(1 << b) | 1 for b in reversed(range(1, bits_of(parts)))] + [1]:
            one = one + lax.ppermute(one, "mp", [(i, i ^ mask) for i in range(parts)])
        return one

    def exchange(value, mask):
        return lax.ppermute(value, "worker", [(w, w ^ mask) for w in range(devices)])

    value = None
    for t in range(iters):
        squared = over_parts(partial)
        relative = t > 0
        got = [[None] * 4 for _ in range(streams)]
        weights = None
        for s in range(streams):
            for r in SEND[s]:
                source = value[s][r] if relative else center
                if weights is None:
                    sent, weights, keep = weigh_first(s, r, source, relative, t, squared)
                else:
                    sent = weigh(s, r, source, relative, weights, keep)
                got[s][r] = exchange(sent, r)
        hold = []
        for s in range(streams):
            own = weigh(s, 0, value[s][0] if relative else center, relative, weights, keep)
            hold.append((own + got[s][1]) + (got[s][2] + got[s][3]))
        for k in range(1, levels - 1):
            for s in range(streams):
                other = exchange(hold[s], 2 << k)
                hold[s] = hold[s] + other
        value = [[hold[s]] + [None] * 3 for s in range(streams)]
        for s in range(streams):
            for r in BACK[s]:
                value[s][r] = exchange(hold[s], r)
        if t + 1 < iters:
            partial = None
            for i in range(4):
                for s in range(streams):
                    r = ((0,) + BACK[s])[i]
                    one = squares(s, r, value[s][r], t + 1 if partial is None else None)
                    partial = one if partial is None else partial + one

    norms = jnp.sqrt(jnp.sum(squared, axis=1))
    final = []
    for s in range(streams):
        tree = value[s]
        for k in range(2):
            turned = (lax.axis_index("worker") >> k) & 1 == 1
            tree = [
                jnp.where(turned, jnp.concatenate([b, a]), jnp.concatenate([a, b]))
                for a, b in zip(tree[0::2], tree[1::2])
            ]
        final.append(tree[0])
    return jnp.concatenate(final).reshape(size), norms


def solution(mesh):
    placed = (P("worker", "mp"), P("mp"), P(None, "worker"), P())

    return jax.shard_map(shards, mesh=mesh, in_specs=placed, out_specs=(P("mp"), P("worker")), check_vma=False)
```

profile of v0, /device:TPU:0, one launch (start us, length us, event | category | flops | bytes accessed | tf_op | source)
XLA Modules:
  0.0 140.7 jit_solution(8394050992843432856)
XLA Ops:
  0.6 4.2 %load.1 = (bf16[2,16384,128]{2,1,0:T(8,128)(2,1)S(1)}, f32[2048,128]{1,0:T(8,128)S(1)}, f32[16,128]{1,0:T(8,128)S(1)}, f32[3,16,128]{2,1,0:T(8,128)S(1)}) custom-call(bf16[2,16384,128]{2,1,0:T(8,128)(2,1)} %bitcast.8, f32[2048,128]{1,0:T(8,128)} %bitcast.9, f32[3,16]{1,0:T(4,128)} %out_hbm.1), custom_call_target="tpu_custom_call" | custom-call | tf_op jit(solution)/shard_map/load/pallas_call | solution.py:188
  4.8 2.5 %collective-permute-start = (f32[16,128]{1,0:T(8,128)S(1)}, f32[16,128]{1,0:T(8,128)S(1)}, u32[]{:S(2)}, u32[]{:S(2)}) collective-permute-start(f32[16,128]{1,0:T(8,128)S(1)} %get-tuple-element.17), channel_id=1, source_target_pairs={{0,3},{1,2},{2,1},{3,0},{4,7},{5,6},{6,5},{7,4},{8,11},{9,10},{10,... | collective-permute-start | bytes 24584 | tf_op jit(solution)/shard_map/ppermute | solution.py:235
  11.8 2.1 %collective-permute-start.2 = (f32[256,128]{1,0:T(8,128)S(1)}, f32[256,128]{1,0:T(8,128)S(1)}, u32[]{:S(2)}, u32[]{:S(2)}) collective-permute-start(f32[256,128]{1,0:T(8,128)S(1)} %weigh.22), channel_id=1, source_target_pairs={{0,4},{4,0},{8,12},{12,8},{16,20},{20,16},{24,28},{28,24},{1,5},{5... | collective-permute-start | bytes 393224 | tf_op jit(solution)/shard_map/ppermute | solution.py:239
  17.1 2.0 %collective-permute-start.7 = (f32[256,128]{1,0:T(8,128)S(1)}, f32[256,128]{1,0:T(8,128)S(1)}, u32[]{:S(2)}, u32[]{:S(2)}) collective-permute-start(f32[256,128]{1,0:T(8,128)S(1)} %weigh.25), channel_id=1, source_target_pairs={{0,4},{4,0},{8,12},{12,8},{16,20},{20,16},{24,28},{28,24},{1,5},{5... | collective-permute-start | bytes 393224 | tf_op jit(solution)/shard_map/ppermute | solution.py:239
  22.3 2.9 %collective-permute-start.5 = (f32[256,128]{1,0:T(8,128)S(1)}, f32[256,128]{1,0:T(8,128)S(1)}, u32[]{:S(2)}, u32[]{:S(2)}) collective-permute-start(f32[256,128]{1,0:T(8,128)S(1)} %add_add_fusion.5), channel_id=1, source_target_pairs={{0,16},{4,20},{8,24},{12,28},{16,0},{20,4},{24,8},{28,12},{1,17},{... | collective-permute-start | bytes 393224 | tf_op jit(solution)/shard_map/ppermute | solution.py:239
  25.1 1.9 %collective-permute-done.7 = f32[256,128]{1,0:T(8,128)S(1)} collective-permute-done((f32[256,128]{1,0:T(8,128)S(1)}, f32[256,128]{1,0:T(8,128)S(1)}, u32[]{:S(2)}, u32[]{:S(2)}) %collective-permute-start.7) | collective-permute-done | bytes 131104 | tf_op jit(solution)/shard_map/ppermute | solution.py:239
  27.5 3.0 %collective-permute-done.8 = f32[256,128]{1,0:T(8,128)S(1)} collective-permute-done((f32[256,128]{1,0:T(8,128)S(1)}, f32[256,128]{1,0:T(8,128)S(1)}, u32[]{:S(2)}, u32[]{:S(2)}) %collective-permute-start.8) | collective-permute-done | bytes 131104 | tf_op jit(solution)/shard_map/ppermute | solution.py:239
  31.7 2.8 %collective-permute-start.6 = (f32[256,128]{1,0:T(8,128)S(1)}, f32[256,128]{1,0:T(8,128)S(1)}, u32[]{:S(2)}, u32[]{:S(2)}) collective-permute-start(f32[256,128]{1,0:T(8,128)S(1)} %add.137.v_ref), channel_id=1, source_target_pairs={{0,12},{4,8},{8,4},{12,0},{16,28},{20,24},{24,20},{28,16},{1,13},{... | collective-permute-start | bytes 393224 | tf_op jit(solution)/shard_map/ppermute | solution.py:239
  34.5 4.2 %collective-permute-done.10 = f32[256,128]{1,0:T(8,128)S(1)} collective-permute-done((f32[256,128]{1,0:T(8,128)S(1)}, f32[256,128]{1,0:T(8,128)S(1)}, u32[]{:S(2)}, u32[]{:S(2)}) %collective-permute-start.10) | collective-permute-done | bytes 131104 | tf_op jit(solution)/shard_map/ppermute | solution.py:239
  43.9 2.2 %collective-permute-done.11.v_ref = f32[256,128]{1,0:T(8,128)S(1)} collective-permute-done((f32[256,128]{1,0:T(8,128)S(1)}, f32[256,128]{1,0:T(8,128)S(1)}, u32[]{:S(2)}, u32[]{:S(2)}) %collective-permute-start.11) | collective-permute-done | bytes 131104 | tf_op jit(solution)/shard_map/ppermute | solution.py:239
  50.8 2.8 %collective-permute-done.16 = f32[16,128]{1,0:T(8,128)S(1)} collective-permute-done((f32[16,128]{1,0:T(8,128)S(1)}, f32[16,128]{1,0:T(8,128)S(1)}, u32[]{:S(2)}, u32[]{:S(2)}) %collective-permute-start.16) | collective-permute-done | bytes 8224 | tf_op jit(solution)/shard_map/ppermute | solution.py:235
  58.2 1.8 %collective-permute-start.20 = (f32[256,128]{1,0:T(8,128)S(1)}, f32[256,128]{1,0:T(8,128)S(1)}, u32[]{:S(2)}, u32[]{:S(2)}) collective-permute-start(f32[256,128]{1,0:T(8,128)S(1)} %get-tuple-element.24), channel_id=1, source_target_pairs={{0,12},{4,8},{8,4},{12,0},{16,28},{20,24},{24,20},{28,16},{1,13},{... | collective-permute-start | bytes 393224 | tf_op jit(solution)/shard_map/ppermute | solution.py:239
  63.3 2.0 %collective-permute-start.24 = (f32[256,128]{1,0:T(8,128)S(1)}, f32[256,128]{1,0:T(8,128)S(1)}, u32[]{:S(2)}, u32[]{:S(2)}) collective-permute-start(f32[256,128]{1,0:T(8,128)S(1)} %weigh.33), channel_id=1, source_target_pairs={{0,8},{4,12},{8,0},{12,4},{16,24},{20,28},{24,16},{28,20},{1,9},{5... | collective-permute-start | bytes 393224 | tf_op jit(solution)/shard_map/ppermute | solution.py:239
  65.3 2.0 %collective-permute-done.20 = f32[256,128]{1,0:T(8,128)S(1)} collective-permute-done((f32[256,128]{1,0:T(8,128)S(1)}, f32[256,128]{1,0:T(8,128)S(1)}, u32[]{:S(2)}, u32[]{:S(2)}) %collective-permute-start.20) | collective-permute-done | bytes 131104 | tf_op jit(solution)/shard_map/ppermute | solution.py:239
  67.9 2.7 %collective-permute-done.23 = f32[256,128]{1,0:T(8,128)S(1)} collective-permute-done((f32[256,128]{1,0:T(8,128)S(1)}, f32[256,128]{1,0:T(8,128)S(1)}, u32[]{:S(2)}, u32[]{:S(2)}) %collective-permute-start.23) | collective-permute-done | bytes 131104 | tf_op jit(solution)/shard_map/ppermute | solution.py:239
  71.4 1.7 %collective-permute-done.24 = f32[256,128]{1,0:T(8,128)S(1)} collective-permute-done((f32[256,128]{1,0:T(8,128)S(1)}, f32[256,128]{1,0:T(8,128)S(1)}, u32[]{:S(2)}, u32[]{:S(2)}) %collective-permute-start.24) | collective-permute-done | bytes 131104 | tf_op jit(solution)/shard_map/ppermute | solution.py:239
  74.5 3.5 %collective-permute-done.21 = f32[256,128]{1,0:T(8,128)S(1)} collective-permute-done((f32[256,128]{1,0:T(8,128)S(1)}, f32[256,128]{1,0:T(8,128)S(1)}, u32[]{:S(2)}, u32[]{:S(2)}) %collective-permute-start.21) | collective-permute-done | bytes 131104 | tf_op jit(solution)/shard_map/ppermute | solution.py:239
  78.9 2.7 %collective-permute-done.26 = f32[256,128]{1,0:T(8,128)S(1)} collective-permute-done((f32[256,128]{1,0:T(8,128)S(1)}, f32[256,128]{1,0:T(8,128)S(1)}, u32[]{:S(2)}, u32[]{:S(2)}) %collective-permute-start.26) | collective-permute-done | bytes 131104 | tf_op jit(solution)/shard_map/ppermute | solution.py:239
  83.7 1.8 %collective-permute-start.30 = (f32[256,128]{1,0:T(8,128)S(1)}, f32[256,128]{1,0:T(8,128)S(1)}, u32[]{:S(2)}, u32[]{:S(2)}) collective-permute-start(f32[256,128]{1,0:T(8,128)S(1)} %add.154.v_ref), channel_id=1, source_target_pairs={{0,8},{4,12},{8,0},{12,4},{16,24},{20,28},{24,16},{28,20},{1,9},{5... | collective-permute-start | bytes 393224 | tf_op jit(solution)/shard_map/ppermute | solution.py:239
  86.7 2.2 %collective-permute-done.27.v_ref = f32[256,128]{1,0:T(8,128)S(1)} collective-permute-done((f32[256,128]{1,0:T(8,128)S(1)}, f32[256,128]{1,0:T(8,128)S(1)}, u32[]{:S(2)}, u32[]{:S(2)}) %collective-permute-start.27) | collective-permute-done | bytes 131104 | tf_op jit(solution)/shard_map/ppermute | solution.py:239
  90.5 1.9 %collective-permute-done.29.v_ref = f32[256,128]{1,0:T(8,128)S(1)} collective-permute-done((f32[256,128]{1,0:T(8,128)S(1)}, f32[256,128]{1,0:T(8,128)S(1)}, u32[]{:S(2)}, u32[]{:S(2)}) %collective-permute-start.29) | collective-permute-done | bytes 131104 | tf_op jit(solution)/shard_map/ppermute | solution.py:239
  94.0 2.5 %collective-permute-done.32 = f32[16,128]{1,0:T(8,128)S(1)} collective-permute-done((f32[16,128]{1,0:T(8,128)S(1)}, f32[16,128]{1,0:T(8,128)S(1)}, u32[]{:S(2)}, u32[]{:S(2)}) %collective-permute-start.32) | collective-permute-done | bytes 8224 | tf_op jit(solution)/shard_map/ppermute | solution.py:235
  101.0 2.1 %collective-permute-start.36 = (f32[256,128]{1,0:T(8,128)S(1)}, f32[256,128]{1,0:T(8,128)S(1)}, u32[]{:S(2)}, u32[]{:S(2)}) collective-permute-start(f32[256,128]{1,0:T(8,128)S(1)} %get-tuple-element.27), channel_id=1, source_target_pairs={{0,12},{4,8},{8,4},{12,0},{16,28},{20,24},{24,20},{28,16},{1,13},{... | collective-permute-start | bytes 393224 | tf_op jit(solution)/shard_map/ppermute | solution.py:239
  106.3 2.0 %collective-permute-start.42 = (f32[256,128]{1,0:T(8,128)S(1)}, f32[256,128]{1,0:T(8,128)S(1)}, u32[]{:S(2)}, u32[]{:S(2)}) collective-permute-start(f32[256,128]{1,0:T(8,128)S(1)} %weigh.40), channel_id=1, source_target_pairs={{0,8},{4,12},{8,0},{12,4},{16,24},{20,28},{24,16},{28,20},{1,9},{5... | collective-permute-start | bytes 393224 | tf_op jit(solution)/shard_map/ppermute | solution.py:239
  108.4 2.0 %collective-permute-done.36 = f32[256,128]{1,0:T(8,128)S(1)} collective-permute-done((f32[256,128]{1,0:T(8,128)S(1)}, f32[256,128]{1,0:T(8,128)S(1)}, u32[]{:S(2)}, u32[]{:S(2)}) %collective-permute-start.36) | collective-permute-done | bytes 131104 | tf_op jit(solution)/shard_map/ppermute | solution.py:239
  111.6 2.0 %collective-permute-done.41 = f32[256,128]{1,0:T(8,128)S(1)} collective-permute-done((f32[256,128]{1,0:T(8,128)S(1)}, f32[256,128]{1,0:T(8,128)S(1)}, u32[]{:S(2)}, u32[]{:S(2)}) %collective-permute-start.41) | collective-permute-done | bytes 131104 | tf_op jit(solution)/shard_map/ppermute | solution.py:239
  117.0 5.4 %collective-permute-done.37 = f32[256,128]{1,0:T(8,128)S(1)} collective-permute-done((f32[256,128]{1,0:T(8,128)S(1)}, f32[256,128]{1,0:T(8,128)S(1)}, u32[]{:S(2)}, u32[]{:S(2)}) %collective-permute-start.37) | collective-permute-done | bytes 131104 | tf_op jit(solution)/shard_map/ppermute | solution.py:239
  122.5 2.0 %collective-permute-done.44 = f32[256,128]{1,0:T(8,128)S(1)} collective-permute-done((f32[256,128]{1,0:T(8,128)S(1)}, f32[256,128]{1,0:T(8,128)S(1)}, u32[]{:S(2)}, u32[]{:S(2)}) %collective-permute-start.44) | collective-permute-done | bytes 131104 | tf_op jit(solution)/shard_map/ppermute | solution.py:239
  125.6 3.0 %collective-permute-start.39 = (f32[256,128]{1,0:T(8,128)S(1)}, f32[256,128]{1,0:T(8,128)S(1)}, u32[]{:S(2)}, u32[]{:S(2)}) collective-permute-start(f32[256,128]{1,0:T(8,128)S(1)} %add.171), channel_id=1, source_target_pairs={{0,8},{4,12},{8,0},{12,4},{16,24},{20,28},{24,16},{28,20},{1,9},{5... | collective-permute-start | bytes 393224 | tf_op jit(solution)/shard_map/ppermute | solution.py:239
  130.5 3.9 %collective-permute-done.47 = f32[256,128]{1,0:T(8,128)S(1)} collective-permute-done((f32[256,128]{1,0:T(8,128)S(1)}, f32[256,128]{1,0:T(8,128)S(1)}, u32[]{:S(2)}, u32[]{:S(2)}) %collective-permute-start.47) | collective-permute-done | bytes 131104 | tf_op jit(solution)/shard_map/ppermute | solution.py:239
  135.8 2.1 %collective-permute-done.45 = f32[256,128]{1,0:T(8,128)S(1)} collective-permute-done((f32[256,128]{1,0:T(8,128)S(1)}, f32[256,128]{1,0:T(8,128)S(1)}, u32[]{:S(2)}, u32[]{:S(2)}) %collective-permute-start.45) | collective-permute-done | bytes 131104 | tf_op jit(solution)/shard_map/ppermute | solution.py:239
  137.9 1.6 %collective-permute-done.46 = f32[256,128]{1,0:T(8,128)S(1)} collective-permute-done((f32[256,128]{1,0:T(8,128)S(1)}, f32[256,128]{1,0:T(8,128)S(1)}, u32[]{:S(2)}, u32[]{:S(2)}) %collective-permute-start.46) | collective-permute-done | bytes 131104 | tf_op jit(solution)/shard_map/ppermute | solution.py:239
  (135 shorter events, 58.1 us)
Async XLA Ops:
  11.8 8.8 %collective-permute-start.2 = (f32[256,128]{1,0:T(8,128)S(1)}, f32[256,128]{1,0:T(8,128)S(1)}, u32[]{:S(2)}, u32[]{:S(2)}) collective-permute-start(f32[256,128]{1,0:T(8,128)S(1)} %weigh.22), channel_id=1, source_target_pairs={{0,4},{4,0},{8,12},{12,8},{16,20},{20,16},{24,28},{28,24},{1,5},{5... | collective-permute-start | bytes 393224 | tf_op jit(solution)/shard_map/ppermute | solution.py:239
  17.1 10.0 %collective-permute-start.7 = (f32[256,128]{1,0:T(8,128)S(1)}, f32[256,128]{1,0:T(8,128)S(1)}, u32[]{:S(2)}, u32[]{:S(2)}) collective-permute-start(f32[256,128]{1,0:T(8,128)S(1)} %weigh.25), channel_id=1, source_target_pairs={{0,4},{4,0},{8,12},{12,8},{16,20},{20,16},{24,28},{28,24},{1,5},{5... | collective-permute-start | bytes 393224 | tf_op jit(solution)/shard_map/ppermute | solution.py:239
  19.0 8.4 %collective-permute-start.9 = (f32[256,128]{1,0:T(8,128)S(1)}, f32[256,128]{1,0:T(8,128)S(1)}, u32[]{:S(2)}, u32[]{:S(2)}) collective-permute-start(f32[256,128]{1,0:T(8,128)S(1)} %weigh.27), channel_id=1, source_target_pairs={{0,12},{4,8},{8,4},{12,0},{16,28},{20,24},{24,20},{28,16},{1,13},{... | collective-permute-start | bytes 393224 | tf_op jit(solution)/shard_map/ppermute | solution.py:239
  20.6 9.9 %collective-permute-start.8 = (f32[256,128]{1,0:T(8,128)S(1)}, f32[256,128]{1,0:T(8,128)S(1)}, u32[]{:S(2)}, u32[]{:S(2)}) collective-permute-start(f32[256,128]{1,0:T(8,128)S(1)} %weigh.26), channel_id=1, source_target_pairs={{0,8},{4,12},{8,0},{12,4},{16,24},{20,28},{24,16},{28,20},{1,9},{5... | collective-permute-start | bytes 393224 | tf_op jit(solution)/shard_map/ppermute | solution.py:239
  22.3 9.5 %collective-permute-start.5 = (f32[256,128]{1,0:T(8,128)S(1)}, f32[256,128]{1,0:T(8,128)S(1)}, u32[]{:S(2)}, u32[]{:S(2)}) collective-permute-start(f32[256,128]{1,0:T(8,128)S(1)} %add_add_fusion.5), channel_id=1, source_target_pairs={{0,16},{4,20},{8,24},{12,28},{16,0},{20,4},{24,8},{28,12},{1,17},{... | collective-permute-start | bytes 393224 | tf_op jit(solution)/shard_map/ppermute | solution.py:239
  30.5 8.2 %collective-permute-start.10 = (f32[256,128]{1,0:T(8,128)S(1)}, f32[256,128]{1,0:T(8,128)S(1)}, u32[]{:S(2)}, u32[]{:S(2)}) collective-permute-start(f32[256,128]{1,0:T(8,128)S(1)} %add_add_fusion.4), channel_id=1, source_target_pairs={{0,16},{4,20},{8,24},{12,28},{16,0},{20,4},{24,8},{28,12},{1,17},{... | collective-permute-start | bytes 393224 | tf_op jit(solution)/shard_map/ppermute | solution.py:239
  31.7 10.7 %collective-permute-start.6 = (f32[256,128]{1,0:T(8,128)S(1)}, f32[256,128]{1,0:T(8,128)S(1)}, u32[]{:S(2)}, u32[]{:S(2)}) collective-permute-start(f32[256,128]{1,0:T(8,128)S(1)} %add.137.v_ref), channel_id=1, source_target_pairs={{0,12},{4,8},{8,4},{12,0},{16,28},{20,24},{24,20},{28,16},{1,13},{... | collective-permute-start | bytes 393224 | tf_op jit(solution)/shard_map/ppermute | solution.py:239
  38.8 8.8 %collective-permute-start.12 = (f32[256,128]{1,0:T(8,128)S(1)}, f32[256,128]{1,0:T(8,128)S(1)}, u32[]{:S(2)}, u32[]{:S(2)}) collective-permute-start(f32[256,128]{1,0:T(8,128)S(1)} %add.137.v_ref), channel_id=1, source_target_pairs={{0,4},{4,0},{8,12},{12,8},{16,20},{20,16},{24,28},{28,24},{1,5},{5... | collective-permute-start | bytes 393224 | tf_op jit(solution)/shard_map/ppermute | solution.py:239
  39.9 9.6 %collective-permute-start.13 = (f32[256,128]{1,0:T(8,128)S(1)}, f32[256,128]{1,0:T(8,128)S(1)}, u32[]{:S(2)}, u32[]{:S(2)}) collective-permute-start(f32[256,128]{1,0:T(8,128)S(1)} %add.141.v_ref), channel_id=1, source_target_pairs={{0,4},{4,0},{8,12},{12,8},{16,20},{20,16},{24,28},{28,24},{1,5},{5... | collective-permute-start | bytes 393224 | tf_op jit(solution)/shard_map/ppermute | solution.py:239
  40.9 8.9 %collective-permute-start.14 = (f32[256,128]{1,0:T(8,128)S(1)}, f32[256,128]{1,0:T(8,128)S(1)}, u32[]{:S(2)}, u32[]{:S(2)}) collective-permute-start(f32[256,128]{1,0:T(8,128)S(1)} %add.137.v_ref), channel_id=1, source_target_pairs={{0,8},{4,12},{8,0},{12,4},{16,24},{20,28},{24,16},{28,20},{1,9},{5... | collective-permute-start | bytes 393224 | tf_op jit(solution)/shard_map/ppermute | solution.py:239
  57.3 8.0 %collective-permute-start.19 = (f32[256,128]{1,0:T(8,128)S(1)}, f32[256,128]{1,0:T(8,128)S(1)}, u32[]{:S(2)}, u32[]{:S(2)}) collective-permute-start(f32[256,128]{1,0:T(8,128)S(1)} %weigh.30), channel_id=1, source_target_pairs={{0,8},{4,12},{8,0},{12,4},{16,24},{20,28},{24,16},{28,20},{1,9},{5... | collective-permute-start | bytes 393224 | tf_op jit(solution)/shard_map/ppermute | solution.py:239
  58.2 9.1 %collective-permute-start.20 = (f32[256,128]{1,0:T(8,128)S(1)}, f32[256,128]{1,0:T(8,128)S(1)}, u32[]{:S(2)}, u32[]{:S(2)}) collective-permute-start(f32[256,128]{1,0:T(8,128)S(1)} %get-tuple-element.24), channel_id=1, source_target_pairs={{0,12},{4,8},{8,4},{12,0},{16,28},{20,24},{24,20},{28,16},{1,13},{... | collective-permute-start | bytes 393224 | tf_op jit(solution)/shard_map/ppermute | solution.py:239
  61.0 9.6 %collective-permute-start.23 = (f32[256,128]{1,0:T(8,128)S(1)}, f32[256,128]{1,0:T(8,128)S(1)}, u32[]{:S(2)}, u32[]{:S(2)}) collective-permute-start(f32[256,128]{1,0:T(8,128)S(1)} %weigh.32), channel_id=1, source_target_pairs={{0,4},{4,0},{8,12},{12,8},{16,20},{20,16},{24,28},{28,24},{1,5},{5... | collective-permute-start | bytes 393224 | tf_op jit(solution)/shard_map/ppermute | solution.py:239
  62.1 9.3 %collective-permute-start.25 = (f32[256,128]{1,0:T(8,128)S(1)}, f32[256,128]{1,0:T(8,128)S(1)}, u32[]{:S(2)}, u32[]{:S(2)}) collective-permute-start(f32[256,128]{1,0:T(8,128)S(1)} %weigh.34), channel_id=1, source_target_pairs={{0,12},{4,8},{8,4},{12,0},{16,28},{20,24},{24,20},{28,16},{1,13},{... | collective-permute-start | bytes 393224 | tf_op jit(solution)/shard_map/ppermute | solution.py:239
  63.3 9.8 %collective-permute-start.24 = (f32[256,128]{1,0:T(8,128)S(1)}, f32[256,128]{1,0:T(8,128)S(1)}, u32[]{:S(2)}, u32[]{:S(2)}) collective-permute-start(f32[256,128]{1,0:T(8,128)S(1)} %weigh.33), channel_id=1, source_target_pairs={{0,8},{4,12},{8,0},{12,4},{16,24},{20,28},{24,16},{28,20},{1,9},{5... | collective-permute-start | bytes 393224 | tf_op jit(solution)/shard_map/ppermute | solution.py:239
  67.3 10.7 %collective-permute-start.21 = (f32[256,128]{1,0:T(8,128)S(1)}, f32[256,128]{1,0:T(8,128)S(1)}, u32[]{:S(2)}, u32[]{:S(2)}) collective-permute-start(f32[256,128]{1,0:T(8,128)S(1)} %add_add_fusion.3), channel_id=1, source_target_pairs={{0,16},{4,20},{8,24},{12,28},{16,0},{20,4},{24,8},{28,12},{1,17},{... | collective-permute-start | bytes 393224 | tf_op jit(solution)/shard_map/ppermute | solution.py:239
  73.1 8.4 %collective-permute-start.26 = (f32[256,128]{1,0:T(8,128)S(1)}, f32[256,128]{1,0:T(8,128)S(1)}, u32[]{:S(2)}, u32[]{:S(2)}) collective-permute-start(f32[256,128]{1,0:T(8,128)S(1)} %add_add_fusion.2), channel_id=1, source_target_pairs={{0,16},{4,20},{8,24},{12,28},{16,0},{20,4},{24,8},{28,12},{1,17},{... | collective-permute-start | bytes 393224 | tf_op jit(solution)/shard_map/ppermute | solution.py:239
  81.6 8.6 %collective-permute-start.28 = (f32[256,128]{1,0:T(8,128)S(1)}, f32[256,128]{1,0:T(8,128)S(1)}, u32[]{:S(2)}, u32[]{:S(2)}) collective-permute-start(f32[256,128]{1,0:T(8,128)S(1)} %add.154.v_ref), channel_id=1, source_target_pairs={{0,4},{4,0},{8,12},{12,8},{16,20},{20,16},{24,28},{28,24},{1,5},{5... | collective-permute-start | bytes 393224 | tf_op jit(solution)/shard_map/ppermute | solution.py:239
  82.7 9.7 %collective-permute-start.29 = (f32[256,128]{1,0:T(8,128)S(1)}, f32[256,128]{1,0:T(8,128)S(1)}, u32[]{:S(2)}, u32[]{:S(2)}) collective-permute-start(f32[256,128]{1,0:T(8,128)S(1)} %add.158.v_ref), channel_id=1, source_target_pairs={{0,4},{4,0},{8,12},{12,8},{16,20},{20,16},{24,28},{28,24},{1,5},{5... | collective-permute-start | bytes 393224 | tf_op jit(solution)/shard_map/ppermute | solution.py:239
  83.7 9.0 %collective-permute-start.30 = (f32[256,128]{1,0:T(8,128)S(1)}, f32[256,128]{1,0:T(8,128)S(1)}, u32[]{:S(2)}, u32[]{:S(2)}) collective-permute-start(f32[256,128]{1,0:T(8,128)S(1)} %add.154.v_ref), channel_id=1, source_target_pairs={{0,8},{4,12},{8,0},{12,4},{16,24},{20,28},{24,16},{28,20},{1,9},{5... | collective-permute-start | bytes 393224 | tf_op jit(solution)/shard_map/ppermute | solution.py:239
  100.1 8.2 %collective-permute-start.35 = (f32[256,128]{1,0:T(8,128)S(1)}, f32[256,128]{1,0:T(8,128)S(1)}, u32[]{:S(2)}, u32[]{:S(2)}) collective-permute-start(f32[256,128]{1,0:T(8,128)S(1)} %weigh.37), channel_id=1, source_target_pairs={{0,8},{4,12},{8,0},{12,4},{16,24},{20,28},{24,16},{28,20},{1,9},{5... | collective-permute-start | bytes 393224 | tf_op jit(solution)/shard_map/ppermute | solution.py:239
  101.0 9.4 %collective-permute-start.36 = (f32[256,128]{1,0:T(8,128)S(1)}, f32[256,128]{1,0:T(8,128)S(1)}, u32[]{:S(2)}, u32[]{:S(2)}) collective-permute-start(f32[256,128]{1,0:T(8,128)S(1)} %get-tuple-element.27), channel_id=1, source_target_pairs={{0,12},{4,8},{8,4},{12,0},{16,28},{20,24},{24,20},{28,16},{1,13},{... | collective-permute-start | bytes 393224 | tf_op jit(solution)/shard_map/ppermute | solution.py:239
  104.0 9.6 %collective-permute-start.41 = (f32[256,128]{1,0:T(8,128)S(1)}, f32[256,128]{1,0:T(8,128)S(1)}, u32[]{:S(2)}, u32[]{:S(2)}) collective-permute-start(f32[256,128]{1,0:T(8,128)S(1)} %weigh.39), channel_id=1, source_target_pairs={{0,4},{4,0},{8,12},{12,8},{16,20},{20,16},{24,28},{28,24},{1,5},{5... | collective-permute-start | bytes 393224 | tf_op jit(solution)/shard_map/ppermute | solution.py:239
  105.0 9.5 %collective-permute-start.43 = (f32[256,128]{1,0:T(8,128)S(1)}, f32[256,128]{1,0:T(8,128)S(1)}, u32[]{:S(2)}, u32[]{:S(2)}) collective-permute-start(f32[256,128]{1,0:T(8,128)S(1)} %weigh.41), channel_id=1, source_target_pairs={{0,12},{4,8},{8,4},{12,0},{16,28},{20,24},{24,20},{28,16},{1,13},{... | collective-permute-start | bytes 393224 | tf_op jit(solution)/shard_map/ppermute | solution.py:239
  106.3 9.4 %collective-permute-start.42 = (f32[256,128]{1,0:T(8,128)S(1)}, f32[256,128]{1,0:T(8,128)S(1)}, u32[]{:S(2)}, u32[]{:S(2)}) collective-permute-start(f32[256,128]{1,0:T(8,128)S(1)} %weigh.40), channel_id=1, source_target_pairs={{0,8},{4,12},{8,0},{12,4},{16,24},{20,28},{24,16},{28,20},{1,9},{5... | collective-permute-start | bytes 393224 | tf_op jit(solution)/shard_map/ppermute | solution.py:239
  110.4 12.0 %collective-permute-start.37 = (f32[256,128]{1,0:T(8,128)S(1)}, f32[256,128]{1,0:T(8,128)S(1)}, u32[]{:S(2)}, u32[]{:S(2)}) collective-permute-start(f32[256,128]{1,0:T(8,128)S(1)} %add_add_fusion.1), channel_id=1, source_target_pairs={{0,16},{4,20},{8,24},{12,28},{16,0},{20,4},{24,8},{28,12},{1,17},{... | collective-permute-start | bytes 393224 | tf_op jit(solution)/shard_map/ppermute | solution.py:239
  115.8 8.7 %collective-permute-start.44 = (f32[256,128]{1,0:T(8,128)S(1)}, f32[256,128]{1,0:T(8,128)S(1)}, u32[]{:S(2)}, u32[]{:S(2)}) collective-permute-start(f32[256,128]{1,0:T(8,128)S(1)} %add_add_fusion), channel_id=1, source_target_pairs={{0,16},{4,20},{8,24},{12,28},{16,0},{20,4},{24,8},{28,12},{1,17},{... | collective-permute-start | bytes 393224 | tf_op jit(solution)/shard_map/ppermute | solution.py:239
  124.5 9.9 %collective-permute-start.47 = (f32[256,128]{1,0:T(8,128)S(1)}, f32[256,128]{1,0:T(8,128)S(1)}, u32[]{:S(2)}, u32[]{:S(2)}) collective-permute-start(f32[256,128]{1,0:T(8,128)S(1)} %add.175), channel_id=1, source_target_pairs={{0,4},{4,0},{8,12},{12,8},{16,20},{20,16},{24,28},{28,24},{1,5},{5... | collective-permute-start | bytes 393224 | tf_op jit(solution)/shard_map/ppermute | solution.py:239
  125.6 8.9 %collective-permute-start.38 = (f32[256,128]{1,0:T(8,128)S(1)}, f32[256,128]{1,0:T(8,128)S(1)}, u32[]{:S(2)}, u32[]{:S(2)}) collective-permute-start(f32[256,128]{1,0:T(8,128)S(1)} %add.171), channel_id=1, source_target_pairs={{0,12},{4,8},{8,4},{12,0},{16,28},{20,24},{24,20},{28,16},{1,13},{... | collective-permute-start | bytes 393224 | tf_op jit(solution)/shard_map/ppermute | solution.py:239
  125.6 10.2 %collective-permute-start.39 = (f32[256,128]{1,0:T(8,128)S(1)}, f32[256,128]{1,0:T(8,128)S(1)}, u32[]{:S(2)}, u32[]{:S(2)}) collective-permute-start(f32[256,128]{1,0:T(8,128)S(1)} %add.171), channel_id=1, source_target_pairs={{0,8},{4,12},{8,0},{12,4},{16,24},{20,28},{24,16},{28,20},{1,9},{5... | collective-permute-start | bytes 393224 | tf_op jit(solution)/shard_map/ppermute | solution.py:239
  128.6 9.3 %collective-permute-start.45 = (f32[256,128]{1,0:T(8,128)S(1)}, f32[256,128]{1,0:T(8,128)S(1)}, u32[]{:S(2)}, u32[]{:S(2)}) collective-permute-start(f32[256,128]{1,0:T(8,128)S(1)} %add.175), channel_id=1, source_target_pairs={{0,12},{4,8},{8,4},{12,0},{16,28},{20,24},{24,20},{28,16},{1,13},{... | collective-permute-start | bytes 393224 | tf_op jit(solution)/shard_map/ppermute | solution.py:239
  129.8 9.8 %collective-permute-start.46 = (f32[256,128]{1,0:T(8,128)S(1)}, f32[256,128]{1,0:T(8,128)S(1)}, u32[]{:S(2)}, u32[]{:S(2)}) collective-permute-start(f32[256,128]{1,0:T(8,128)S(1)} %add.175), channel_id=1, source_target_pairs={{0,8},{4,12},{8,0},{12,4},{16,24},{20,28},{24,16},{28,20},{1,9},{5... | collective-permute-start | bytes 393224 | tf_op jit(solution)/shard_map/ppermute | solution.py:239
  (17 other events, 96.0 us)
where the time goes:
time: 141 us
  waiting for transfers between devices  68 us (48%)
  starting transfers between devices  51 us (36%)
  Pallas kernels  18.5 us (13%)
  other arithmetic  1.61 us (1%)
    ppermute x42, waiting for transfers between devices, exchange(): lax.ppermute(value, 'worker', [(w, w ^ mask) for w in range(devices)])  58.4 us
    ppermute x42, starting transfers between devices, exchange(): lax.ppermute(value, 'worker', [(w, w ^ mask) for w in range(devices)])  46.6 us
    ppermute x6, waiting for transfers between devices, over_parts(): one = one + lax.ppermute(one, 'mp', [(i, i ^ mask) for i in range(parts)])  9.61 us
    pallas_call x21, Pallas kernels, weigh(): pl.pallas_call(functools.partial(weigh_body, functools.partial(offset, s,...  6.43 us
    pallas_call x16, Pallas kernels, squares(): pl.pallas_call(functools.partial(square_body, functools.partial(offset, s...  4.83 us
    ppermute x6, starting transfers between devices, over_parts(): one = one + lax.ppermute(one, 'mp', [(i, i ^ mask) for i in range(parts)])  4.34 us
    pallas_call x1, Pallas kernels, shards(): pl.pallas_call(functools.partial(load_body, chunks, parts), out_shape=(ja...  4.19 us
    pallas_call x3, Pallas kernels, weigh_first(): pl.pallas_call(body, out_shape=(quarter_shape(s), weight_shape, keep_shap...  3.02 us
  transfers between devices with their start and end apart: 48, of which 34 were waited for; matrix products, arithmetic and copies ran while one was open for 1% of the time, Pallas kernels for 7%

commit v1 on v0

--- a/solution.py
+++ b/solution.py
@@ -98,28 +98,22 @@
 
 def build_weights(root, workers, devices, groups, s_ref, w_ref, k_ref):
     depth = BLOCK * GROUP
-    ones = jnp.ones((GROUP, LANES), jnp.bfloat16)
     block = lax.broadcasted_iota(jnp.int32, (BLOCK, depth), 0)
     place = lax.broadcasted_iota(jnp.int32, (BLOCK, depth), 1)
+    lane = lax.broadcasted_iota(jnp.int32, (GROUP, depth), 1)
+    sub = lax.broadcasted_iota(jnp.int32, (GROUP, depth), 0)
     total = None
     for g in range(groups):
-        one = s_ref[g * GROUP:(g + 1) * GROUP, :]
-        two = jnp.concatenate([one, one], axis=0)
-        high = two.astype(jnp.bfloat16)
-        low = (two - high.astype(jnp.float32)).astype(jnp.bfloat16)
-        squared = None
-        for half in (high, low):
-            tall = jnp.concatenate([half] * (BLOCK // 2), axis=0)
-            part = lax.dot_general(ones, tall, (((1,), (1,)), ((), ())), preferred_element_type=jnp.float32)
-            squared = part if squared is None else squared + part
+        squared = jnp.sum(s_ref[g * GROUP:(g + 1) * GROUP, :], axis=1, keepdims=True)
         factor = jnp.minimum(jnp.float32(1.0), root / jnp.sqrt(squared))
         total = factor if total is None else total + factor
-        factor = factor[0:1] / jnp.float32(workers)
+        factor = jnp.where(lane % GROUP == sub, factor, 0.0)
+        factor = jnp.sum(factor, axis=0, keepdims=True) / jnp.float32(workers)
         high = factor.astype(jnp.bfloat16).astype(jnp.float32)
         low = factor - high
         for h, half in enumerate((high, low)):
             w_ref[g, h * BLOCK:(h + 1) * BLOCK, :] = jnp.where(place // GROUP == block, half, 0.0).astype(jnp.bfloat16)
-    share = jnp.sum(total, axis=1, keepdims=True) / jnp.float32(BLOCK * workers)
+    share = jnp.sum(total, axis=0, keepdims=True) / jnp.float32(workers)
     k_ref[...] = jnp.broadcast_to(jnp.float32(1.0 / devices) - share, k_ref.shape)
 
 

time: 141 us -> 140 us (level)
  no operation moved by 1% of the time
where the time goes in v1:
time: 140 us
  waiting for transfers between devices  68 us (49%)
  starting transfers between devices  51 us (36%)
  Pallas kernels  18.1 us (13%)
  other arithmetic  1.61 us (1%)
    ppermute x42, waiting for transfers between devices, exchange(): lax.ppermute(value, 'worker', [(w, w ^ mask) for w in range(devices)])  58.4 us
    ppermute x42, starting transfers between devices, exchange(): lax.ppermute(value, 'worker', [(w, w ^ mask) for w in range(devices)])  46.6 us
    ppermute x6, waiting for transfers between devices, over_parts(): one = one + lax.ppermute(one, 'mp', [(i, i ^ mask) for i in range(parts)])  9.62 us
    pallas_call x21, Pallas kernels, weigh(): pl.pallas_call(functools.partial(weigh_body, functools.partial(offset, s,...  6.43 us
    pallas_call x16, Pallas kernels, squares(): pl.pallas_call(functools.partial(square_body, functools.partial(offset, s...  4.83 us
    ppermute x6, starting transfers between devices, over_parts(): one = one + lax.ppermute(one, 'mp', [(i, i ^ mask) for i in range(parts)])  4.34 us
    pallas_call x1, Pallas kernels, shards(): pl.pallas_call(functools.partial(load_body, chunks, parts), out_shape=(ja...  4.19 us
  transfers between devices with their start and end apart: 48, of which 34 were waited for; matrix products, arithmetic and copies ran while one was open for 1% of the time, Pallas kernels for 7%

profile of v1, /device:TPU:0, one launch (start us, length us, event | category | flops | bytes accessed | tf_op | source)
XLA Modules:
  0.0 140.3 jit_solution(881345856873945383)
XLA Ops:
  0.6 4.2 %load.1 = (bf16[2,16384,128]{2,1,0:T(8,128)(2,1)S(1)}, f32[2048,128]{1,0:T(8,128)S(1)}, f32[16,128]{1,0:T(8,128)S(1)}, f32[3,16,128]{2,1,0:T(8,128)S(1)}) custom-call(bf16[2,16384,128]{2,1,0:T(8,128)(2,1)} %bitcast.8, f32[2048,128]{1,0:T(8,128)} %bitcast.9, f32[3,16]{1,0:T(4,128)} %out_hbm.1), custom_call_target="tpu_custom_call" | custom-call | tf_op jit(solution)/shard_map/load/pallas_call | solution.py:182
  4.8 2.5 %collective-permute-start = (f32[16,128]{1,0:T(8,128)S(1)}, f32[16,128]{1,0:T(8,128)S(1)}, u32[]{:S(2)}, u32[]{:S(2)}) collective-permute-start(f32[16,128]{1,0:T(8,128)S(1)} %get-tuple-element.17), channel_id=1, source_target_pairs={{0,3},{1,2},{2,1},{3,0},{4,7},{5,6},{6,5},{7,4},{8,11},{9,10},{10,... | collective-permute-start | bytes 24584 | tf_op jit(solution)/shard_map/ppermute | solution.py:229
  11.7 2.1 %collective-permute-start.2 = (f32[256,128]{1,0:T(8,128)S(1)}, f32[256,128]{1,0:T(8,128)S(1)}, u32[]{:S(2)}, u32[]{:S(2)}) collective-permute-start(f32[256,128]{1,0:T(8,128)S(1)} %weigh.22), channel_id=1, source_target_pairs={{0,4},{4,0},{8,12},{12,8},{16,20},{20,16},{24,28},{28,24},{1,5},{5... | collective-permute-start | bytes 393224 | tf_op jit(solution)/shard_map/ppermute | solution.py:233
  17.0 2.0 %collective-permute-start.7 = (f32[256,128]{1,0:T(8,128)S(1)}, f32[256,128]{1,0:T(8,128)S(1)}, u32[]{:S(2)}, u32[]{:S(2)}) collective-permute-start(f32[256,128]{1,0:T(8,128)S(1)} %weigh.25), channel_id=1, source_target_pairs={{0,4},{4,0},{8,12},{12,8},{16,20},{20,16},{24,28},{28,24},{1,5},{5... | collective-permute-start | bytes 393224 | tf_op jit(solution)/shard_map/ppermute | solution.py:233
  22.1 2.9 %collective-permute-start.5 = (f32[256,128]{1,0:T(8,128)S(1)}, f32[256,128]{1,0:T(8,128)S(1)}, u32[]{:S(2)}, u32[]{:S(2)}) collective-permute-start(f32[256,128]{1,0:T(8,128)S(1)} %add_add_fusion.5), channel_id=1, source_target_pairs={{0,16},{4,20},{8,24},{12,28},{16,0},{20,4},{24,8},{28,12},{1,17},{... | collective-permute-start | bytes 393224 | tf_op jit(solution)/shard_map/ppermute | solution.py:233
  25.0 1.9 %collective-permute-done.7 = f32[256,128]{1,0:T(8,128)S(1)} collective-permute-done((f32[256,128]{1,0:T(8,128)S(1)}, f32[256,128]{1,0:T(8,128)S(1)}, u32[]{:S(2)}, u32[]{:S(2)}) %collective-permute-start.7) | collective-permute-done | bytes 131104 | tf_op jit(solution)/shard_map/ppermute | solution.py:233
  27.4 3.0 %collective-permute-done.8 = f32[256,128]{1,0:T(8,128)S(1)} collective-permute-done((f32[256,128]{1,0:T(8,128)S(1)}, f32[256,128]{1,0:T(8,128)S(1)}, u32[]{:S(2)}, u32[]{:S(2)}) %collective-permute-start.8) | collective-permute-done | bytes 131104 | tf_op jit(solution)/shard_map/ppermute | solution.py:233
  31.6 2.8 %collective-permute-start.6 = (f32[256,128]{1,0:T(8,128)S(1)}, f32[256,128]{1,0:T(8,128)S(1)}, u32[]{:S(2)}, u32[]{:S(2)}) collective-permute-start(f32[256,128]{1,0:T(8,128)S(1)} %add.137.v_ref), channel_id=1, source_target_pairs={{0,12},{4,8},{8,4},{12,0},{16,28},{20,24},{24,20},{28,16},{1,13},{... | collective-permute-start | bytes 393224 | tf_op jit(solution)/shard_map/ppermute | solution.py:233
  34.4 4.2 %collective-permute-done.10 = f32[256,128]{1,0:T(8,128)S(1)} collective-permute-done((f32[256,128]{1,0:T(8,128)S(1)}, f32[256,128]{1,0:T(8,128)S(1)}, u32[]{:S(2)}, u32[]{:S(2)}) %collective-permute-start.10) | collective-permute-done | bytes 131104 | tf_op jit(solution)/shard_map/ppermute | solution.py:233
  43.8 2.2 %collective-permute-done.11.v_ref = f32[256,128]{1,0:T(8,128)S(1)} collective-permute-done((f32[256,128]{1,0:T(8,128)S(1)}, f32[256,128]{1,0:T(8,128)S(1)}, u32[]{:S(2)}, u32[]{:S(2)}) %collective-permute-start.11) | collective-permute-done | bytes 131104 | tf_op jit(solution)/shard_map/ppermute | solution.py:233
  50.7 2.8 %collective-permute-done.16 = f32[16,128]{1,0:T(8,128)S(1)} collective-permute-done((f32[16,128]{1,0:T(8,128)S(1)}, f32[16,128]{1,0:T(8,128)S(1)}, u32[]{:S(2)}, u32[]{:S(2)}) %collective-permute-start.16) | collective-permute-done | bytes 8224 | tf_op jit(solution)/shard_map/ppermute | solution.py:229
  58.0 1.8 %collective-permute-start.20 = (f32[256,128]{1,0:T(8,128)S(1)}, f32[256,128]{1,0:T(8,128)S(1)}, u32[]{:S(2)}, u32[]{:S(2)}) collective-permute-start(f32[256,128]{1,0:T(8,128)S(1)} %get-tuple-element.24), channel_id=1, source_target_pairs={{0,12},{4,8},{8,4},{12,0},{16,28},{20,24},{24,20},{28,16},{1,13},{... | collective-permute-start | bytes 393224 | tf_op jit(solution)/shard_map/ppermute | solution.py:233
  63.1 2.0 %collective-permute-start.24 = (f32[256,128]{1,0:T(8,128)S(1)}, f32[256,128]{1,0:T(8,128)S(1)}, u32[]{:S(2)}, u32[]{:S(2)}) collective-permute-start(f32[256,128]{1,0:T(8,128)S(1)} %weigh.33), channel_id=1, source_target_pairs={{0,8},{4,12},{8,0},{12,4},{16,24},{20,28},{24,16},{28,20},{1,9},{5... | collective-permute-start | bytes 393224 | tf_op jit(solution)/shard_map/ppermute | solution.py:233
  65.1 2.0 %collective-permute-done.20 = f32[256,128]{1,0:T(8,128)S(1)} collective-permute-done((f32[256,128]{1,0:T(8,128)S(1)}, f32[256,128]{1,0:T(8,128)S(1)}, u32[]{:S(2)}, u32[]{:S(2)}) %collective-permute-start.20) | collective-permute-done | bytes 131104 | tf_op jit(solution)/shard_map/ppermute | solution.py:233
  67.7 2.6 %collective-permute-done.23 = f32[256,128]{1,0:T(8,128)S(1)} collective-permute-done((f32[256,128]{1,0:T(8,128)S(1)}, f32[256,128]{1,0:T(8,128)S(1)}, u32[]{:S(2)}, u32[]{:S(2)}) %collective-permute-start.23) | collective-permute-done | bytes 131104 | tf_op jit(solution)/shard_map/ppermute | solution.py:233
  71.2 1.7 %collective-permute-done.24 = f32[256,128]{1,0:T(8,128)S(1)} collective-permute-done((f32[256,128]{1,0:T(8,128)S(1)}, f32[256,128]{1,0:T(8,128)S(1)}, u32[]{:S(2)}, u32[]{:S(2)}) %collective-permute-start.24) | collective-permute-done | bytes 131104 | tf_op jit(solution)/shard_map/ppermute | solution.py:233
  74.3 3.5 %collective-permute-done.21 = f32[256,128]{1,0:T(8,128)S(1)} collective-permute-done((f32[256,128]{1,0:T(8,128)S(1)}, f32[256,128]{1,0:T(8,128)S(1)}, u32[]{:S(2)}, u32[]{:S(2)}) %collective-permute-start.21) | collective-permute-done | bytes 131104 | tf_op jit(solution)/shard_map/ppermute | solution.py:233
  78.6 2.6 %collective-permute-done.26 = f32[256,128]{1,0:T(8,128)S(1)} collective-permute-done((f32[256,128]{1,0:T(8,128)S(1)}, f32[256,128]{1,0:T(8,128)S(1)}, u32[]{:S(2)}, u32[]{:S(2)}) %collective-permute-start.26) | collective-permute-done | bytes 131104 | tf_op jit(solution)/shard_map/ppermute | solution.py:233
  83.5 1.8 %collective-permute-start.30 = (f32[256,128]{1,0:T(8,128)S(1)}, f32[256,128]{1,0:T(8,128)S(1)}, u32[]{:S(2)}, u32[]{:S(2)}) collective-permute-start(f32[256,128]{1,0:T(8,128)S(1)} %add.154.v_ref), channel_id=1, source_target_pairs={{0,8},{4,12},{8,0},{12,4},{16,24},{20,28},{24,16},{28,20},{1,9},{5... | collective-permute-start | bytes 393224 | tf_op jit(solution)/shard_map/ppermute | solution.py:233
  86.4 2.2 %collective-permute-done.27.v_ref = f32[256,128]{1,0:T(8,128)S(1)} collective-permute-done((f32[256,128]{1,0:T(8,128)S(1)}, f32[256,128]{1,0:T(8,128)S(1)}, u32[]{:S(2)}, u32[]{:S(2)}) %collective-permute-start.27) | collective-permute-done | bytes 131104 | tf_op jit(solution)/shard_map/ppermute | solution.py:233
  90.3 1.9 %collective-permute-done.29.v_ref = f32[256,128]{1,0:T(8,128)S(1)} collective-permute-done((f32[256,128]{1,0:T(8,128)S(1)}, f32[256,128]{1,0:T(8,128)S(1)}, u32[]{:S(2)}, u32[]{:S(2)}) %collective-permute-start.29) | collective-permute-done | bytes 131104 | tf_op jit(solution)/shard_map/ppermute | solution.py:233
  93.8 2.6 %collective-permute-done.32 = f32[16,128]{1,0:T(8,128)S(1)} collective-permute-done((f32[16,128]{1,0:T(8,128)S(1)}, f32[16,128]{1,0:T(8,128)S(1)}, u32[]{:S(2)}, u32[]{:S(2)}) %collective-permute-start.32) | collective-permute-done | bytes 8224 | tf_op jit(solution)/shard_map/ppermute | solution.py:229
  100.6 2.1 %collective-permute-start.36 = (f32[256,128]{1,0:T(8,128)S(1)}, f32[256,128]{1,0:T(8,128)S(1)}, u32[]{:S(2)}, u32[]{:S(2)}) collective-permute-start(f32[256,128]{1,0:T(8,128)S(1)} %get-tuple-element.27), channel_id=1, source_target_pairs={{0,12},{4,8},{8,4},{12,0},{16,28},{20,24},{24,20},{28,16},{1,13},{... | collective-permute-start | bytes 393224 | tf_op jit(solution)/shard_map/ppermute | solution.py:233
  106.0 2.0 %collective-permute-start.42 = (f32[256,128]{1,0:T(8,128)S(1)}, f32[256,128]{1,0:T(8,128)S(1)}, u32[]{:S(2)}, u32[]{:S(2)}) collective-permute-start(f32[256,128]{1,0:T(8,128)S(1)} %weigh.40), channel_id=1, source_target_pairs={{0,8},{4,12},{8,0},{12,4},{16,24},{20,28},{24,16},{28,20},{1,9},{5... | collective-permute-start | bytes 393224 | tf_op jit(solution)/shard_map/ppermute | solution.py:233
  108.0 2.0 %collective-permute-done.36 = f32[256,128]{1,0:T(8,128)S(1)} collective-permute-done((f32[256,128]{1,0:T(8,128)S(1)}, f32[256,128]{1,0:T(8,128)S(1)}, u32[]{:S(2)}, u32[]{:S(2)}) %collective-permute-start.36) | collective-permute-done | bytes 131104 | tf_op jit(solution)/shard_map/ppermute | solution.py:233
  111.3 2.0 %collective-permute-done.41 = f32[256,128]{1,0:T(8,128)S(1)} collective-permute-done((f32[256,128]{1,0:T(8,128)S(1)}, f32[256,128]{1,0:T(8,128)S(1)}, u32[]{:S(2)}, u32[]{:S(2)}) %collective-permute-start.41) | collective-permute-done | bytes 131104 | tf_op jit(solution)/shard_map/ppermute | solution.py:233
  116.7 5.4 %collective-permute-done.37 = f32[256,128]{1,0:T(8,128)S(1)} collective-permute-done((f32[256,128]{1,0:T(8,128)S(1)}, f32[256,128]{1,0:T(8,128)S(1)}, u32[]{:S(2)}, u32[]{:S(2)}) %collective-permute-start.37) | collective-permute-done | bytes 131104 | tf_op jit(solution)/shard_map/ppermute | solution.py:233
  122.2 2.0 %collective-permute-done.44 = f32[256,128]{1,0:T(8,128)S(1)} collective-permute-done((f32[256,128]{1,0:T(8,128)S(1)}, f32[256,128]{1,0:T(8,128)S(1)}, u32[]{:S(2)}, u32[]{:S(2)}) %collective-permute-start.44) | collective-permute-done | bytes 131104 | tf_op jit(solution)/shard_map/ppermute | solution.py:233
  125.3 2.9 %collective-permute-start.39 = (f32[256,128]{1,0:T(8,128)S(1)}, f32[256,128]{1,0:T(8,128)S(1)}, u32[]{:S(2)}, u32[]{:S(2)}) collective-permute-start(f32[256,128]{1,0:T(8,128)S(1)} %add.171), channel_id=1, source_target_pairs={{0,8},{4,12},{8,0},{12,4},{16,24},{20,28},{24,16},{28,20},{1,9},{5... | collective-permute-start | bytes 393224 | tf_op jit(solution)/shard_map/ppermute | solution.py:233
  130.3 3.4 %collective-permute-done.47 = f32[256,128]{1,0:T(8,128)S(1)} collective-permute-done((f32[256,128]{1,0:T(8,128)S(1)}, f32[256,128]{1,0:T(8,128)S(1)}, u32[]{:S(2)}, u32[]{:S(2)}) %collective-permute-start.47) | collective-permute-done | bytes 131104 | tf_op jit(solution)/shard_map/ppermute | solution.py:233
  133.7 1.7 %collective-permute-done.39 = f32[256,128]{1,0:T(8,128)S(1)} collective-permute-done((f32[256,128]{1,0:T(8,128)S(1)}, f32[256,128]{1,0:T(8,128)S(1)}, u32[]{:S(2)}, u32[]{:S(2)}) %collective-permute-start.39) | collective-permute-done | bytes 131104 | tf_op jit(solution)/shard_map/ppermute | solution.py:233
  135.5 2.4 %collective-permute-done.45 = f32[256,128]{1,0:T(8,128)S(1)} collective-permute-done((f32[256,128]{1,0:T(8,128)S(1)}, f32[256,128]{1,0:T(8,128)S(1)}, u32[]{:S(2)}, u32[]{:S(2)}) %collective-permute-start.45) | collective-permute-done | bytes 131104 | tf_op jit(solution)/shard_map/ppermute | solution.py:233
  (135 shorter events, 58.1 us)
Async XLA Ops:
  11.7 8.8 %collective-permute-start.2 = (f32[256,128]{1,0:T(8,128)S(1)}, f32[256,128]{1,0:T(8,128)S(1)}, u32[]{:S(2)}, u32[]{:S(2)}) collective-permute-start(f32[256,128]{1,0:T(8,128)S(1)} %weigh.22), channel_id=1, source_target_pairs={{0,4},{4,0},{8,12},{12,8},{16,20},{20,16},{24,28},{28,24},{1,5},{5... | collective-permute-start | bytes 393224 | tf_op jit(solution)/shard_map/ppermute | solution.py:233
  17.0 10.0 %collective-permute-start.7 = (f32[256,128]{1,0:T(8,128)S(1)}, f32[256,128]{1,0:T(8,128)S(1)}, u32[]{:S(2)}, u32[]{:S(2)}) collective-permute-start(f32[256,128]{1,0:T(8,128)S(1)} %weigh.25), channel_id=1, source_target_pairs={{0,4},{4,0},{8,12},{12,8},{16,20},{20,16},{24,28},{28,24},{1,5},{5... | collective-permute-start | bytes 393224 | tf_op jit(solution)/shard_map/ppermute | solution.py:233
  18.9 8.4 %collective-permute-start.9 = (f32[256,128]{1,0:T(8,128)S(1)}, f32[256,128]{1,0:T(8,128)S(1)}, u32[]{:S(2)}, u32[]{:S(2)}) collective-permute-start(f32[256,128]{1,0:T(8,128)S(1)} %weigh.27), channel_id=1, source_target_pairs={{0,12},{4,8},{8,4},{12,0},{16,28},{20,24},{24,20},{28,16},{1,13},{... | collective-permute-start | bytes 393224 | tf_op jit(solution)/shard_map/ppermute | solution.py:233
  20.5 9.9 %collective-permute-start.8 = (f32[256,128]{1,0:T(8,128)S(1)}, f32[256,128]{1,0:T(8,128)S(1)}, u32[]{:S(2)}, u32[]{:S(2)}) collective-permute-start(f32[256,128]{1,0:T(8,128)S(1)} %weigh.26), channel_id=1, source_target_pairs={{0,8},{4,12},{8,0},{12,4},{16,24},{20,28},{24,16},{28,20},{1,9},{5... | collective-permute-start | bytes 393224 | tf_op jit(solution)/shard_map/ppermute | solution.py:233
  22.1 9.5 %collective-permute-start.5 = (f32[256,128]{1,0:T(8,128)S(1)}, f32[256,128]{1,0:T(8,128)S(1)}, u32[]{:S(2)}, u32[]{:S(2)}) collective-permute-start(f32[256,128]{1,0:T(8,128)S(1)} %add_add_fusion.5), channel_id=1, source_target_pairs={{0,16},{4,20},{8,24},{12,28},{16,0},{20,4},{24,8},{28,12},{1,17},{... | collective-permute-start | bytes 393224 | tf_op jit(solution)/shard_map/ppermute | solution.py:233
  30.4 8.2 %collective-permute-start.10 = (f32[256,128]{1,0:T(8,128)S(1)}, f32[256,128]{1,0:T(8,128)S(1)}, u32[]{:S(2)}, u32[]{:S(2)}) collective-permute-start(f32[256,128]{1,0:T(8,128)S(1)} %add_add_fusion.4), channel_id=1, source_target_pairs={{0,16},{4,20},{8,24},{12,28},{16,0},{20,4},{24,8},{28,12},{1,17},{... | collective-permute-start | bytes 393224 | tf_op jit(solution)/shard_map/ppermute | solution.py:233
  31.6 10.7 %collective-permute-start.6 = (f32[256,128]{1,0:T(8,128)S(1)}, f32[256,128]{1,0:T(8,128)S(1)}, u32[]{:S(2)}, u32[]{:S(2)}) collective-permute-start(f32[256,128]{1,0:T(8,128)S(1)} %add.137.v_ref), channel_id=1, source_target_pairs={{0,12},{4,8},{8,4},{12,0},{16,28},{20,24},{24,20},{28,16},{1,13},{... | collective-permute-start | bytes 393224 | tf_op jit(solution)/shard_map/ppermute | solution.py:233
  38.7 8.8 %collective-permute-start.12 = (f32[256,128]{1,0:T(8,128)S(1)}, f32[256,128]{1,0:T(8,128)S(1)}, u32[]{:S(2)}, u32[]{:S(2)}) collective-permute-start(f32[256,128]{1,0:T(8,128)S(1)} %add.137.v_ref), channel_id=1, source_target_pairs={{0,4},{4,0},{8,12},{12,8},{16,20},{20,16},{24,28},{28,24},{1,5},{5... | collective-permute-start | bytes 393224 | tf_op jit(solution)/shard_map/ppermute | solution.py:233
  39.8 9.6 %collective-permute-start.13 = (f32[256,128]{1,0:T(8,128)S(1)}, f32[256,128]{1,0:T(8,128)S(1)}, u32[]{:S(2)}, u32[]{:S(2)}) collective-permute-start(f32[256,128]{1,0:T(8,128)S(1)} %add.141.v_ref), channel_id=1, source_target_pairs={{0,4},{4,0},{8,12},{12,8},{16,20},{20,16},{24,28},{28,24},{1,5},{5... | collective-permute-start | bytes 393224 | tf_op jit(solution)/shard_map/ppermute | solution.py:233
  40.8 8.9 %collective-permute-start.14 = (f32[256,128]{1,0:T(8,128)S(1)}, f32[256,128]{1,0:T(8,128)S(1)}, u32[]{:S(2)}, u32[]{:S(2)}) collective-permute-start(f32[256,128]{1,0:T(8,128)S(1)} %add.137.v_ref), channel_id=1, source_target_pairs={{0,8},{4,12},{8,0},{12,4},{16,24},{20,28},{24,16},{28,20},{1,9},{5... | collective-permute-start | bytes 393224 | tf_op jit(solution)/shard_map/ppermute | solution.py:233
  57.0 8.0 %collective-permute-start.19 = (f32[256,128]{1,0:T(8,128)S(1)}, f32[256,128]{1,0:T(8,128)S(1)}, u32[]{:S(2)}, u32[]{:S(2)}) collective-permute-start(f32[256,128]{1,0:T(8,128)S(1)} %weigh.30), channel_id=1, source_target_pairs={{0,8},{4,12},{8,0},{12,4},{16,24},{20,28},{24,16},{28,20},{1,9},{5... | collective-permute-start | bytes 393224 | tf_op jit(solution)/shard_map/ppermute | solution.py:233
  58.0 9.1 %collective-permute-start.20 = (f32[256,128]{1,0:T(8,128)S(1)}, f32[256,128]{1,0:T(8,128)S(1)}, u32[]{:S(2)}, u32[]{:S(2)}) collective-permute-start(f32[256,128]{1,0:T(8,128)S(1)} %get-tuple-element.24), channel_id=1, source_target_pairs={{0,12},{4,8},{8,4},{12,0},{16,28},{20,24},{24,20},{28,16},{1,13},{... | collective-permute-start | bytes 393224 | tf_op jit(solution)/shard_map/ppermute | solution.py:233
  60.7 9.6 %collective-permute-start.23 = (f32[256,128]{1,0:T(8,128)S(1)}, f32[256,128]{1,0:T(8,128)S(1)}, u32[]{:S(2)}, u32[]{:S(2)}) collective-permute-start(f32[256,128]{1,0:T(8,128)S(1)} %weigh.32), channel_id=1, source_target_pairs={{0,4},{4,0},{8,12},{12,8},{16,20},{20,16},{24,28},{28,24},{1,5},{5... | collective-permute-start | bytes 393224 | tf_op jit(solution)/shard_map/ppermute | solution.py:233
  61.9 9.3 %collective-permute-start.25 = (f32[256,128]{1,0:T(8,128)S(1)}, f32[256,128]{1,0:T(8,128)S(1)}, u32[]{:S(2)}, u32[]{:S(2)}) collective-permute-start(f32[256,128]{1,0:T(8,128)S(1)} %weigh.34), channel_id=1, source_target_pairs={{0,12},{4,8},{8,4},{12,0},{16,28},{20,24},{24,20},{28,16},{1,13},{... | collective-permute-start | bytes 393224 | tf_op jit(solution)/shard_map/ppermute | solution.py:233
  63.1 9.8 %collective-permute-start.24 = (f32[256,128]{1,0:T(8,128)S(1)}, f32[256,128]{1,0:T(8,128)S(1)}, u32[]{:S(2)}, u32[]{:S(2)}) collective-permute-start(f32[256,128]{1,0:T(8,128)S(1)} %weigh.33), channel_id=1, source_target_pairs={{0,8},{4,12},{8,0},{12,4},{16,24},{20,28},{24,16},{28,20},{1,9},{5... | collective-permute-start | bytes 393224 | tf_op jit(solution)/shard_map/ppermute | solution.py:233
  67.1 10.7 %collective-permute-start.21 = (f32[256,128]{1,0:T(8,128)S(1)}, f32[256,128]{1,0:T(8,128)S(1)}, u32[]{:S(2)}, u32[]{:S(2)}) collective-permute-start(f32[256,128]{1,0:T(8,128)S(1)} %add_add_fusion.3), channel_id=1, source_target_pairs={{0,16},{4,20},{8,24},{12,28},{16,0},{20,4},{24,8},{28,12},{1,17},{... | collective-permute-start | bytes 393224 | tf_op jit(solution)/shard_map/ppermute | solution.py:233
  72.9 8.4 %collective-permute-start.26 = (f32[256,128]{1,0:T(8,128)S(1)}, f32[256,128]{1,0:T(8,128)S(1)}, u32[]{:S(2)}, u32[]{:S(2)}) collective-permute-start(f32[256,128]{1,0:T(8,128)S(1)} %add_add_fusion.2), channel_id=1, source_target_pairs={{0,16},{4,20},{8,24},{12,28},{16,0},{20,4},{24,8},{28,12},{1,17},{... | collective-permute-start | bytes 393224 | tf_op jit(solution)/shard_map/ppermute | solution.py:233
  81.4 8.6 %collective-permute-start.28 = (f32[256,128]{1,0:T(8,128)S(1)}, f32[256,128]{1,0:T(8,128)S(1)}, u32[]{:S(2)}, u32[]{:S(2)}) collective-permute-start(f32[256,128]{1,0:T(8,128)S(1)} %add.154.v_ref), channel_id=1, source_target_pairs={{0,4},{4,0},{8,12},{12,8},{16,20},{20,16},{24,28},{28,24},{1,5},{5... | collective-permute-start | bytes 393224 | tf_op jit(solution)/shard_map/ppermute | solution.py:233
  82.5 9.7 %collective-permute-start.29 = (f32[256,128]{1,0:T(8,128)S(1)}, f32[256,128]{1,0:T(8,128)S(1)}, u32[]{:S(2)}, u32[]{:S(2)}) collective-permute-start(f32[256,128]{1,0:T(8,128)S(1)} %add.158.v_ref), channel_id=1, source_target_pairs={{0,4},{4,0},{8,12},{12,8},{16,20},{20,16},{24,28},{28,24},{1,5},{5... | collective-permute-start | bytes 393224 | tf_op jit(solution)/shard_map/ppermute | solution.py:233
  83.5 9.0 %collective-permute-start.30 = (f32[256,128]{1,0:T(8,128)S(1)}, f32[256,128]{1,0:T(8,128)S(1)}, u32[]{:S(2)}, u32[]{:S(2)}) collective-permute-start(f32[256,128]{1,0:T(8,128)S(1)} %add.154.v_ref), channel_id=1, source_target_pairs={{0,8},{4,12},{8,0},{12,4},{16,24},{20,28},{24,16},{28,20},{1,9},{5... | collective-permute-start | bytes 393224 | tf_op jit(solution)/shard_map/ppermute | solution.py:233
  99.9 8.2 %collective-permute-start.35 = (f32[256,128]{1,0:T(8,128)S(1)}, f32[256,128]{1,0:T(8,128)S(1)}, u32[]{:S(2)}, u32[]{:S(2)}) collective-permute-start(f32[256,128]{1,0:T(8,128)S(1)} %weigh.37), channel_id=1, source_target_pairs={{0,8},{4,12},{8,0},{12,4},{16,24},{20,28},{24,16},{28,20},{1,9},{5... | collective-permute-start | bytes 393224 | tf_op jit(solution)/shard_map/ppermute | solution.py:233
  100.6 9.4 %collective-permute-start.36 = (f32[256,128]{1,0:T(8,128)S(1)}, f32[256,128]{1,0:T(8,128)S(1)}, u32[]{:S(2)}, u32[]{:S(2)}) collective-permute-start(f32[256,128]{1,0:T(8,128)S(1)} %get-tuple-element.27), channel_id=1, source_target_pairs={{0,12},{4,8},{8,4},{12,0},{16,28},{20,24},{24,20},{28,16},{1,13},{... | collective-permute-start | bytes 393224 | tf_op jit(solution)/shard_map/ppermute | solution.py:233
  103.7 9.6 %collective-permute-start.41 = (f32[256,128]{1,0:T(8,128)S(1)}, f32[256,128]{1,0:T(8,128)S(1)}, u32[]{:S(2)}, u32[]{:S(2)}) collective-permute-start(f32[256,128]{1,0:T(8,128)S(1)} %weigh.39), channel_id=1, source_target_pairs={{0,4},{4,0},{8,12},{12,8},{16,20},{20,16},{24,28},{28,24},{1,5},{5... | collective-permute-start | bytes 393224 | tf_op jit(solution)/shard_map/ppermute | solution.py:233
  104.7 9.5 %collective-permute-start.43 = (f32[256,128]{1,0:T(8,128)S(1)}, f32[256,128]{1,0:T(8,128)S(1)}, u32[]{:S(2)}, u32[]{:S(2)}) collective-permute-start(f32[256,128]{1,0:T(8,128)S(1)} %weigh.41), channel_id=1, source_target_pairs={{0,12},{4,8},{8,4},{12,0},{16,28},{20,24},{24,20},{28,16},{1,13},{... | collective-permute-start | bytes 393224 | tf_op jit(solution)/shard_map/ppermute | solution.py:233
  106.0 9.6 %collective-permute-start.42 = (f32[256,128]{1,0:T(8,128)S(1)}, f32[256,128]{1,0:T(8,128)S(1)}, u32[]{:S(2)}, u32[]{:S(2)}) collective-permute-start(f32[256,128]{1,0:T(8,128)S(1)} %weigh.40), channel_id=1, source_target_pairs={{0,8},{4,12},{8,0},{12,4},{16,24},{20,28},{24,16},{28,20},{1,9},{5... | collective-permute-start | bytes 393224 | tf_op jit(solution)/shard_map/ppermute | solution.py:233
  110.1 12.0 %collective-permute-start.37 = (f32[256,128]{1,0:T(8,128)S(1)}, f32[256,128]{1,0:T(8,128)S(1)}, u32[]{:S(2)}, u32[]{:S(2)}) collective-permute-start(f32[256,128]{1,0:T(8,128)S(1)} %add_add_fusion.1), channel_id=1, source_target_pairs={{0,16},{4,20},{8,24},{12,28},{16,0},{20,4},{24,8},{28,12},{1,17},{... | collective-permute-start | bytes 393224 | tf_op jit(solution)/shard_map/ppermute | solution.py:233
  115.6 8.6 %collective-permute-start.44 = (f32[256,128]{1,0:T(8,128)S(1)}, f32[256,128]{1,0:T(8,128)S(1)}, u32[]{:S(2)}, u32[]{:S(2)}) collective-permute-start(f32[256,128]{1,0:T(8,128)S(1)} %add_add_fusion), channel_id=1, source_target_pairs={{0,16},{4,20},{8,24},{12,28},{16,0},{20,4},{24,8},{28,12},{1,17},{... | collective-permute-start | bytes 393224 | tf_op jit(solution)/shard_map/ppermute | solution.py:233
  124.2 9.5 %collective-permute-start.47 = (f32[256,128]{1,0:T(8,128)S(1)}, f32[256,128]{1,0:T(8,128)S(1)}, u32[]{:S(2)}, u32[]{:S(2)}) collective-permute-start(f32[256,128]{1,0:T(8,128)S(1)} %add.175), channel_id=1, source_target_pairs={{0,4},{4,0},{8,12},{12,8},{16,20},{20,16},{24,28},{28,24},{1,5},{5... | collective-permute-start | bytes 393224 | tf_op jit(solution)/shard_map/ppermute | solution.py:233
  125.3 8.4 %collective-permute-start.38 = (f32[256,128]{1,0:T(8,128)S(1)}, f32[256,128]{1,0:T(8,128)S(1)}, u32[]{:S(2)}, u32[]{:S(2)}) collective-permute-start(f32[256,128]{1,0:T(8,128)S(1)} %add.171), channel_id=1, source_target_pairs={{0,12},{4,8},{8,4},{12,0},{16,28},{20,24},{24,20},{28,16},{1,13},{... | collective-permute-start | bytes 393224 | tf_op jit(solution)/shard_map/ppermute | solution.py:233
  125.3 10.1 %collective-permute-start.39 = (f32[256,128]{1,0:T(8,128)S(1)}, f32[256,128]{1,0:T(8,128)S(1)}, u32[]{:S(2)}, u32[]{:S(2)}) collective-permute-start(f32[256,128]{1,0:T(8,128)S(1)} %add.171), channel_id=1, source_target_pairs={{0,8},{4,12},{8,0},{12,4},{16,24},{20,28},{24,16},{28,20},{1,9},{5... | collective-permute-start | bytes 393224 | tf_op jit(solution)/shard_map/ppermute | solution.py:233
  128.3 9.6 %collective-permute-start.45 = (f32[256,128]{1,0:T(8,128)S(1)}, f32[256,128]{1,0:T(8,128)S(1)}, u32[]{:S(2)}, u32[]{:S(2)}) collective-permute-start(f32[256,128]{1,0:T(8,128)S(1)} %add.175), channel_id=1, source_target_pairs={{0,12},{4,8},{8,4},{12,0},{16,28},{20,24},{24,20},{28,16},{1,13},{... | collective-permute-start | bytes 393224 | tf_op jit(solution)/shard_map/ppermute | solution.py:233
  129.5 9.7 %collective-permute-start.46 = (f32[256,128]{1,0:T(8,128)S(1)}, f32[256,128]{1,0:T(8,128)S(1)}, u32[]{:S(2)}, u32[]{:S(2)}) collective-permute-start(f32[256,128]{1,0:T(8,128)S(1)} %add.175), channel_id=1, source_target_pairs={{0,8},{4,12},{8,0},{12,4},{16,24},{20,28},{24,16},{28,20},{1,9},{5... | collective-permute-start | bytes 393224 | tf_op jit(solution)/shard_map/ppermute | solution.py:233
  (17 other events, 96.0 us)
